TPU v7x, 32 devices: a whole 2x2x4 slice. The times are simulated.
32 devices in a mesh: dp: 8 (over z, x), tensor: 4 (over y, core).
Axes of the slice: x: 2, y: 2, z: 4, core: 2. Of those that a mesh axis runs over, the one named last changes fastest.
Arguments:
- segments: bfloat16 [32, 704, 512], P('dp'), may hold values from -6 to 6
- seg_start: int32 [32, 704], P('dp'), may hold values from 0 to 2048, as said below
- seg_count: int32 [32], P('dp'), may hold values from 300 to 704, as said below
- norm_gain: bfloat16 [512], P('dp'), may hold values from 0.25 to 1.75
- norm_shift: bfloat16 [512], P('dp'), may hold values from -3 to 3
- qkv_weight: bfloat16 [512, 3, 512], P('dp', None, 'tensor'), may hold values from -0.25 to 0.25
- out_weight: bfloat16 [512, 512], P(('tensor', 'dp')), may hold values from -1 to 1
- ffn_gain: bfloat16 [512], P('dp'), may hold values from 0.25 to 1.75
- ffn_shift: bfloat16 [512], P('dp'), may hold values from -3 to 3
- up_weight: bfloat16 [512, 2048], P('dp', 'tensor'), may hold values from -0.25 to 0.25
- up_bias: bfloat16 [2048], P(('tensor', 'dp')), may hold values from -3 to 3
- down_weight: bfloat16 [2048, 512], P(('tensor', 'dp')), may hold values from -0.125 to 0.125
- cotangent: bfloat16 [32, 704, 512], P('dp'), may hold values from -6 to 6
Outputs:
- block_out: bfloat16 [32, 704, 512], P('dp')
- segments_grad: float32 [32, 704, 512], P('dp')
- norm_gain_grad: float32 [512], P('dp')
- norm_shift_grad: float32 [512], P('dp')
- qkv_weight_grad: float32 [512, 3, 512], P('dp', None, 'tensor')
- out_weight_grad: float32 [512, 512], P(('tensor', 'dp'))
- ffn_gain_grad: float32 [512], P('dp')
- ffn_shift_grad: float32 [512], P('dp')
- up_weight_grad: float32 [512, 2048], P('dp', 'tensor')
- up_bias_grad: float32 [2048], P(('tensor', 'dp'))
- down_weight_grad: float32 [2048, 512], P(('tensor', 'dp'))
Inputs may be any that keep to these rules, and one draw needn't show every extreme that they name: One sequence has exactly 704 live segments and one exactly 300; slots at and after seg_count are padding. `seg_start`: 0 in the first slot, strictly rising over a sequence's live segments and below 2048 there; 2048 in every padded slot.
All inputs are finite; a program needn't handle non-finite values.
Results may differ from a plain program's by a relative error of at most 0.014.
Values may be sent and summed in bfloat16 or wider, within the bound.
No kernel may reach another device: no remote copies, remote signals or barrier semaphores. Data moves between devices by JAX's collectives and lax.ppermute only.
A program may use at most 128 MiB of HBM per device.

v0:
```python
import math
import jax
import jax.numpy as jnp
from jax import lax
from jax.sharding import PartitionSpec as P

HEAD = 64
EPSILON = 1e-05
MASKED = -1e30


def split_up(array, dim, devices):
    dims = array.shape
    pieces = array.reshape(*dims[:dim], devices, dims[dim] // devices, *dims[dim + 1 :])
    return jnp.moveaxis(pieces, dim, 0)


def summed_on_arrival(array, axis, dim):
    pieces = split_up(array, dim, lax.axis_size(axis))
    arrived = lax.all_to_all(pieces, axis, split_axis=0, concat_axis=0, tiled=True)
    return arrived.astype(jnp.float32).sum(axis=0)


def sent_together(arrays, axis, dim, along):
    widths = [math.prod(a.shape[along:]) for a in arrays]
    both = jnp.concatenate(
        [a.reshape(*a.shape[:along], w) for a, w in zip(arrays, widths)], axis=along
    )
    filled = summed_on_arrival(both, axis, dim)
    pieces = jnp.split(filled, [sum(widths[:k]) for k in range(1, len(widths))], axis=along)
    return tuple(
        (b.reshape(*filled.shape[:along], *a.shape[along:]) for a, b in zip(arrays, pieces))
    )


def normalize(values, scale_vec, offset_vec):
    centre = jnp.mean(values, axis=-1, keepdims=True)
    centred = values - centre
    spread = jnp.mean(centred * centred, axis=-1, keepdims=True)
    return centred * lax.rsqrt(spread + EPSILON) * scale_vec + offset_vec


def rotate(values, cosine, sine_term):
    half_size = values.shape[-1] // 2
    turned = jnp.concatenate([-values[..., half_size:], values[..., :half_size]], axis=-1)
    return values * cosine + turned * sine_term


def rotary_tables(starts, head_size):
    half_size = head_size // 2
    freq_index = jnp.arange(half_size).astype(jnp.float32)
    inverse = jnp.exp(freq_index * (-math.log(10000.0) / half_size))
    angles = starts.astype(jnp.float32)[..., None] * inverse
    angles = jnp.concatenate([angles, angles], axis=-1)
    return (jnp.cos(angles), jnp.sin(angles))


def allowed_keys(length, live_count):
    places = jnp.arange(length)
    return (places[None, :] <= places[:, None]) & (places[None, :] < live_count)


def exact_gelu(values):
    return jax.nn.gelu(values, approximate=False)


def masked_scores(queries, key_rows, live_count):
    scores = jnp.einsum("qhd,khd->hqk", queries, key_rows, preferred_element_type=jnp.float32)
    allowed = allowed_keys(queries.shape[0], live_count)
    return jnp.where(allowed[None], scores, MASKED)


def attend_forward(packed):
    queries, key_rows, value_rows, live_count = packed
    scores = masked_scores(queries, key_rows, live_count)
    row_max = jnp.max(scores, axis=-1, keepdims=True)
    weights = jnp.exp(scores - row_max)
    row_total = jnp.sum(weights, axis=-1, keepdims=True)
    attention_probs = weights / row_total
    mixed_rows = jnp.einsum(
        "hqk,khd->qhd",
        attention_probs.astype(jnp.bfloat16),
        value_rows,
        preferred_element_type=jnp.float32,
    )
    return (mixed_rows.astype(jnp.bfloat16), row_max[..., 0] + jnp.log(row_total[..., 0]))


def attend_backward(packed):
    queries, key_rows, value_rows, live_count, log_total, out_grad = packed
    scores = masked_scores(queries, key_rows, live_count)
    attention_probs = jnp.exp(scores - log_total[..., None])
    prob_grad = jnp.einsum("qhd,khd->hqk", out_grad, value_rows, preferred_element_type=jnp.float32)
    inner_sum = jnp.sum(prob_grad * attention_probs, axis=-1, keepdims=True)
    score_grad = (attention_probs * (prob_grad - inner_sum)).astype(jnp.bfloat16)
    query_grad = jnp.einsum(
        "hqk,khd->qhd", score_grad, key_rows, preferred_element_type=jnp.float32
    )
    key_grad = jnp.einsum("hqk,qhd->khd", score_grad, queries, preferred_element_type=jnp.float32)
    value_grad = jnp.einsum(
        "hqk,qhd->khd",
        attention_probs.astype(jnp.bfloat16),
        out_grad,
        preferred_element_type=jnp.float32,
    )
    return (query_grad, key_grad, value_grad)


def run_layer(segments, seg_start, seg_count, cotangent, weights):
    seq_local, seg_len, model_width = segments.shape
    token_rows = seq_local * seg_len
    gain_one = weights[0].astype(jnp.float32)
    shift_one = weights[1].astype(jnp.float32)
    gain_two = weights[2].astype(jnp.float32)
    shift_two = weights[3].astype(jnp.float32)
    w_qkv, w_out, w_up = (weights[4], weights[5], weights[6])
    b_up = weights[7].astype(jnp.float32)
    w_down = weights[8]
    local_width = w_qkv.shape[2]
    local_heads = local_width // HEAD
    head_shape = (token_rows, local_heads, HEAD)
    seq_shape = (seq_local, seg_len, local_heads, HEAD)
    inputs = segments.reshape(token_rows, model_width).astype(jnp.float32)
    normed_one, norm_one_pull = jax.vjp(normalize, inputs, gain_one, shift_one)
    attn_in = normed_one.astype(jnp.bfloat16)
    projected = jnp.einsum("nd,dct->nct", attn_in, w_qkv, preferred_element_type=jnp.float32)
    cosine, sine_term = rotary_tables(seg_start.reshape(token_rows), HEAD)
    cosine = cosine[:, None, :]
    sine_term = sine_term[:, None, :]

    def place_rotary(raw_query, raw_key):
        return (
            rotate(raw_query, cosine, sine_term) * HEAD ** (-0.5),
            rotate(raw_key, cosine, sine_term),
        )

    rotated, rotary_pull = jax.vjp(
        place_rotary, projected[:, 0].reshape(head_shape), projected[:, 1].reshape(head_shape)
    )
    queries = rotated[0].astype(jnp.bfloat16).reshape(seq_shape)
    key_rows = rotated[1].astype(jnp.bfloat16).reshape(seq_shape)
    value_rows = projected[:, 2].astype(jnp.bfloat16).reshape(seq_shape)
    mixed_rows, log_total = lax.map(attend_forward, (queries, key_rows, value_rows, seg_count))
    mixed_flat = mixed_rows.reshape(token_rows, local_width)
    attn_part = jnp.dot(mixed_flat, w_out, preferred_element_type=jnp.float32)
    attn_full = lax.psum(attn_part, "tensor")
    residual = inputs + attn_full
    normed_two, norm_two_pull = jax.vjp(normalize, residual, gain_two, shift_two)
    ffn_in = normed_two.astype(jnp.bfloat16)
    pre_act = jnp.dot(ffn_in, w_up, preferred_element_type=jnp.float32) + b_up
    activated, gelu_pull = jax.vjp(exact_gelu, pre_act)
    act_low = activated.astype(jnp.bfloat16)
    ffn_part = jnp.dot(act_low, w_down, preferred_element_type=jnp.float32)
    ffn_full = lax.psum(ffn_part.astype(jnp.bfloat16), "tensor").astype(jnp.float32)
    block_out = (residual + ffn_full).astype(jnp.bfloat16).reshape(segments.shape)
    out_rows = cotangent.reshape(token_rows, model_width)
    down_grad = jnp.einsum("nf,nd->fd", act_low, out_rows, preferred_element_type=jnp.float32)
    act_grad = jnp.einsum("nd,fd->nf", out_rows, w_down, preferred_element_type=jnp.float32)
    pre_grad = gelu_pull(act_grad)[0].astype(jnp.bfloat16)
    bias_grad = jnp.sum(pre_grad, axis=0, dtype=jnp.float32)
    up_grad = jnp.einsum("nd,nf->df", ffn_in, pre_grad, preferred_element_type=jnp.float32)
    ffn_in_part = jnp.einsum("nf,df->nd", pre_grad, w_up, preferred_element_type=jnp.float32)
    ffn_in_grad = lax.psum(ffn_in_part, "tensor")
    resid_ln_grad, gain_two_grad, shift_two_grad = norm_two_pull(ffn_in_grad)
    residual_grad = out_rows.astype(jnp.float32) + resid_ln_grad
    attn_grad_low = residual_grad.astype(jnp.bfloat16)
    out_w_grad = jnp.einsum(
        "nt,nd->td", mixed_flat, attn_grad_low, preferred_element_type=jnp.float32
    )
    mixed_grad = jnp.einsum(
        "nd,td->nt", attn_grad_low, w_out, preferred_element_type=jnp.float32
    ).astype(jnp.bfloat16)
    ffn_shares = None
    query_grad, key_grad, value_grad = lax.map(
        attend_backward,
        (queries, key_rows, value_rows, seg_count, log_total, mixed_grad.reshape(seq_shape)),
    )
    raw_query_grad, raw_key_grad = rotary_pull(
        (query_grad.reshape(head_shape), key_grad.reshape(head_shape))
    )
    proj_grad = jnp.stack(
        [
            raw_query_grad.reshape(token_rows, local_width),
            raw_key_grad.reshape(token_rows, local_width),
            value_grad.reshape(token_rows, local_width),
        ],
        axis=1,
    ).astype(jnp.bfloat16)
    qkv_grad = jnp.einsum("nd,nct->dct", attn_in, proj_grad, preferred_element_type=jnp.float32)
    attn_in_part = jnp.einsum("nct,dct->nd", proj_grad, w_qkv, preferred_element_type=jnp.float32)
    attn_in_grad = lax.psum(attn_in_part.astype(jnp.bfloat16), "tensor").astype(jnp.float32)
    input_ln_grad, gain_one_grad, shift_one_grad = norm_one_pull(attn_in_grad)
    input_grad = (residual_grad + input_ln_grad).reshape(segments.shape)
    grads = (
        gain_one_grad,
        shift_one_grad,
        qkv_grad,
        out_w_grad,
        gain_two_grad,
        shift_two_grad,
        up_grad,
        bias_grad,
        down_grad,
    )
    return (block_out, input_grad, grads, ffn_shares)


def local(
    segments,
    seg_start,
    seg_count,
    norm_gain,
    norm_shift,
    qkv_weight,
    out_weight,
    ffn_gain,
    ffn_shift,
    up_weight,
    up_bias,
    down_weight,
    cotangent,
):
    gathered = (
        lax.all_gather(norm_gain, "dp", axis=0, tiled=True),
        lax.all_gather(norm_shift, "dp", axis=0, tiled=True),
        lax.all_gather(ffn_gain, "dp", axis=0, tiled=True),
        lax.all_gather(ffn_shift, "dp", axis=0, tiled=True),
        lax.all_gather(qkv_weight, "dp", axis=0, tiled=True),
        lax.all_gather(out_weight, "dp", axis=0, tiled=True),
        lax.all_gather(up_weight, "dp", axis=0, tiled=True),
        lax.all_gather(up_bias, "dp", axis=0, tiled=True),
        lax.all_gather(down_weight, "dp", axis=0, tiled=True),
    )
    block_out, input_grad, grads, ffn_shares = run_layer(
        segments, seg_start, seg_count, cotangent, gathered
    )
    (
        gain_one_grad,
        shift_one_grad,
        qkv_grad,
        out_w_grad,
        gain_two_grad,
        shift_two_grad,
        up_grad,
        bias_grad,
        down_grad,
    ) = grads
    shares = (
        summed_on_arrival(gain_one_grad.astype(jnp.bfloat16), "dp", 0),
        *sent_together(
            (shift_one_grad.astype(jnp.bfloat16), qkv_grad.astype(jnp.bfloat16)), "dp", 0, 1
        ),
        summed_on_arrival(out_w_grad.astype(jnp.bfloat16), "dp", 0),
        summed_on_arrival(gain_two_grad.astype(jnp.bfloat16), "dp", 0),
        *sent_together(
            (
                shift_two_grad.astype(jnp.bfloat16),
                up_grad.astype(jnp.bfloat16),
                bias_grad.astype(jnp.bfloat16),
                down_grad.astype(jnp.bfloat16),
            ),
            "dp",
            0,
            1,
        ),
    )
    gain_one_s, shift_one_s, qkv_s, out_s, gain_two_s, shift_two_s, up_s, bias_s, down_s = shares
    return (
        block_out,
        input_grad,
        gain_one_s,
        shift_one_s,
        qkv_s,
        out_s,
        gain_two_s,
        shift_two_s,
        up_s,
        bias_s,
        down_s,
    )


def solution(mesh):
    placed = (
        P("dp", None, None),
        P("dp", None),
        P("dp"),
        P("dp"),
        P("dp"),
        P("dp", None, "tensor"),
        P(("tensor", "dp"), None),
        P("dp"),
        P("dp"),
        P("dp", "tensor"),
        P(("tensor", "dp")),
        P(("tensor", "dp"), None),
        P("dp", None, None),
    )
    return jax.shard_map(
        local,
        mesh=mesh,
        in_specs=placed,
        out_specs=(
            P("dp", None, None),
            P("dp", None, None),
            P("dp"),
            P("dp"),
            P("dp", None, "tensor"),
            P(("tensor", "dp"), None),
            P("dp"),
            P("dp"),
            P("dp", "tensor"),
            P(("tensor", "dp")),
            P(("tensor", "dp"), None),
        ),
        check_vma=False,
    )
```

profile of v0, /device:TPU:0, one launch (start us, length us, event | category | flops | bytes accessed | tf_op | source)
XLA Modules:
  0.0 764.0 jit_solution(6756772383985416356)
XLA Ops:
  13.8 23.3 %all-reduce.9 = (bf16[512]{0:T(512)(128)(2,1)S(1)}, bf16[512]{0:T(512)(128)(2,1)S(1)}, bf16[512]{0:T(512)(128)(2,1)S(1)}, bf16[512]{0:T(512)(128)(2,1)S(1)}, bf16[512]{0:T(512)(128)(2,1)S(1)}) all-reduce(bf16[512]{0:T(512)(128)(2,1)S(1)} %dynamic-update-slice.1, ...), channel_id=1, replica_groups=mesh['dp'=8,'tensor'=4] {'dp'}, use_global_device_ids=true, to_apply=%add.5 | all-reduce | flops 2560 | bytes 10240
  37.3 31.0 %all_gather.29 = bf16[512,3,128]{2,0,1:T(8,128)(2,1)S(1)} all-gather(bf16[64,3,128]{2,0,1:T(8,128)(2,1)S(1)} %copy-done.44), channel_id=1, replica_groups=mesh['dp'=8,'tensor'=4] {'dp'}, dimensions={0}, use_global_device_ids=true | all-gather | bytes 442368 | tf_op jit(solution)/shard_map/all_gather | solution.py:228
  74.1 30.7 %all_gather.30 = bf16[128,512]{1,0:T(8,128)(2,1)S(1)} all-gather(bf16[16,512]{1,0:T(8,128)(2,1)S(1)} %copy-done.45), channel_id=1, replica_groups=mesh['dp'=8,'tensor'=4] {'dp'}, dimensions={0}, use_global_device_ids=true | all-gather | bytes 147456 | tf_op jit(solution)/shard_map/all_gather | solution.py:229
  104.9 6.5 fusion.85
  144.9 31.6 %while.26 = (s32[]{:T(128)}, bf16[4,704,2,64]{1,3,2,0:T(8,128)(2,1)}, f32[4,2,704]{2,1,0:T(2,128)}, bf16[4,704,2,64]{1,3,2,0:T(8,128)(2,1)}, s32[4]{0:T(128)S(1)...) while((s32[]{:T(128)}, bf16[4,704,2,64]{1,3,2,0:T(8,128)(2,1)}, ...), condition=%wide.region_5.6_spmd, body=%wide.region_2.5_spmd.sunk | while | flops 263757120 | bytes 14712817 | solution.py:143
  188.4 31.8 %all_gather.33 = bf16[512,512]{1,0:T(8,128)(2,1)S(1)} all-gather(bf16[64,512]{1,0:T(8,128)(2,1)} %param.26), channel_id=1, replica_groups=mesh['dp'=8,'tensor'=4] {'dp'}, dimensions={0}, use_global_device_ids=true | all-gather | bytes 589824 | tf_op jit(solution)/shard_map/all_gather | solution.py:230
  220.2 33.4 %all_gather.35 = bf16[512,512]{1,0:T(8,128)(2,1)} all-gather(bf16[64,512]{1,0:T(8,128)(2,1)} %param.28), channel_id=1, replica_groups=mesh['dp'=8,'tensor'=4] {'dp'}, dimensions={0}, use_global_device_ids=true | all-gather | bytes 589824 | tf_op jit(solution)/shard_map/all_gather | solution.py:232
  253.5 41.4 %all-reduce.15.cloned.1.call-done = f32[2816,512]{1,0:T(8,128)} async-done(((f32[2816,512]{1,0:T(8,128)}), f32[2816,512]{1,0:T(8,128)}) %all-reduce.15.cloned.1.call-update) | async-done | bytes 5767184 | tf_op jit(solution)/shard_map/psum | solution.py:146
  303.4 16.5 %fusion.89 = (bf16[512]{0:T(512)(128)(2,1)}, bf16[2816,512]{1,0:T(8,128)(2,1)S(1)}, f32[2816,512]{1,0:T(8,128)}) fusion(f32[2816,512]{1,0:T(8,128)S(1)} %fusion.98, f32[512]{0:T(512)S(1)} %copy-done.48, bf16[2816,512]{1,0:T(8,128)(2,1)S(1)} %bitcast.198, bf16[512,512]{1,0:T(8,128)(2,1)S(1)} %copy-done.29), kind=kOutput, calls=%fused_computation.166 | convolution fusion | flops 1583087104 | bytes 17828864 | tf_op jit(solution)/shard_map/nd,fd->nf/dot_general | solution.py:158
  330.1 7.0 multiply_convert_fusion.1
  343.1 93.9 %all-reduce.17.cloned.1.call-done = f32[2816,512]{1,0:T(8,128)} async-done(((f32[2816,512]{1,0:T(8,128)}), f32[2816,512]{1,0:T(8,128)}) %all-reduce.17.cloned.1.call-update) | async-done | bytes 5767184 | tf_op jit(solution)/shard_map/psum | solution.py:163
  466.9 106.9 %while.27 = (s32[]{:T(128)}, f32[4,704,2,64]{1,0,3,2:T(4,128)}, f32[4,704,2,64]{1,0,3,2:T(4,128)}, bf16[4,704,2,64]{1,3,2,0:T(8,128)(2,1)}, bf16[4,704,2,64]{1,3...) while((s32[]{:T(128)}, f32[4,704,2,64]{1,0,3,2:T(4,128)}, ...), condition=%wide.region_15.16_spmd, body=%wide.region_13.15_spmd.sunk | while | flops 647273792 | bytes 44077144 | solution.py:174
  476.8 8.4 %dynamic_update_slice.30 = f32[4,704,2,64]{1,0,3,2:T(4,128)} dynamic-update-slice(f32[4,704,2,64]{1,0,3,2:T(4,128)} %get-tuple-element.440, f32[1,704,2,64]{1,0,3,2:T(1,128)S(1)} %copy.151, s32[]{:T(128)S(6)} %copy.177, s32[]{:T(128)} %constant.60.clone.1..sunk, s32[]{:T(128)} %constant.60.clone.1..sunk, s32[]{:T(128)} %constant.60.clone.1..sunk) | dynamic-update-slice | bytes 720900 | tf_op jit(solution)/shard_map/while/body/jit(dynamic_update_index_in_dim)/dynamic_update_slice | solution.py:174
  485.2 8.4 %dynamic_update_slice.29 = f32[4,704,2,64]{1,0,3,2:T(4,128)} dynamic-update-slice(f32[4,704,2,64]{1,0,3,2:T(4,128)} %get-tuple-element.439, f32[1,704,2,64]{1,0,3,2:T(1,128)S(1)} %copy.150, s32[]{:T(128)S(6)} %copy.177, s32[]{:T(128)} %constant.60.clone.1..sunk, s32[]{:T(128)} %constant.60.clone.1..sunk, s32[]{:T(128)} %constant.60.clone.1..sunk) | dynamic-update-slice | bytes 720900 | tf_op jit(solution)/shard_map/while/body/jit(dynamic_update_index_in_dim)/dynamic_update_slice | solution.py:174
  503.5 8.4 %dynamic_update_slice.30 = f32[4,704,2,64]{1,0,3,2:T(4,128)} dynamic-update-slice(f32[4,704,2,64]{1,0,3,2:T(4,128)} %get-tuple-element.440, f32[1,704,2,64]{1,0,3,2:T(1,128)S(1)} %copy.151, s32[]{:T(128)S(6)} %copy.177, s32[]{:T(128)} %constant.60.clone.1..sunk, s32[]{:T(128)} %constant.60.clone.1..sunk, s32[]{:T(128)} %constant.60.clone.1..sunk) | dynamic-update-slice | bytes 720900 | tf_op jit(solution)/shard_map/while/body/jit(dynamic_update_index_in_dim)/dynamic_update_slice | solution.py:174
  511.9 8.4 %dynamic_update_slice.29 = f32[4,704,2,64]{1,0,3,2:T(4,128)} dynamic-update-slice(f32[4,704,2,64]{1,0,3,2:T(4,128)} %get-tuple-element.439, f32[1,704,2,64]{1,0,3,2:T(1,128)S(1)} %copy.150, s32[]{:T(128)S(6)} %copy.177, s32[]{:T(128)} %constant.60.clone.1..sunk, s32[]{:T(128)} %constant.60.clone.1..sunk, s32[]{:T(128)} %constant.60.clone.1..sunk) | dynamic-update-slice | bytes 720900 | tf_op jit(solution)/shard_map/while/body/jit(dynamic_update_index_in_dim)/dynamic_update_slice | solution.py:174
  530.2 8.4 %dynamic_update_slice.30 = f32[4,704,2,64]{1,0,3,2:T(4,128)} dynamic-update-slice(f32[4,704,2,64]{1,0,3,2:T(4,128)} %get-tuple-element.440, f32[1,704,2,64]{1,0,3,2:T(1,128)S(1)} %copy.151, s32[]{:T(128)S(6)} %copy.177, s32[]{:T(128)} %constant.60.clone.1..sunk, s32[]{:T(128)} %constant.60.clone.1..sunk, s32[]{:T(128)} %constant.60.clone.1..sunk) | dynamic-update-slice | bytes 720900 | tf_op jit(solution)/shard_map/while/body/jit(dynamic_update_index_in_dim)/dynamic_update_slice | solution.py:174
  538.6 8.4 %dynamic_update_slice.29 = f32[4,704,2,64]{1,0,3,2:T(4,128)} dynamic-update-slice(f32[4,704,2,64]{1,0,3,2:T(4,128)} %get-tuple-element.439, f32[1,704,2,64]{1,0,3,2:T(1,128)S(1)} %copy.150, s32[]{:T(128)S(6)} %copy.177, s32[]{:T(128)} %constant.60.clone.1..sunk, s32[]{:T(128)} %constant.60.clone.1..sunk, s32[]{:T(128)} %constant.60.clone.1..sunk) | dynamic-update-slice | bytes 720900 | tf_op jit(solution)/shard_map/while/body/jit(dynamic_update_index_in_dim)/dynamic_update_slice | solution.py:174
  556.9 8.4 %dynamic_update_slice.30 = f32[4,704,2,64]{1,0,3,2:T(4,128)} dynamic-update-slice(f32[4,704,2,64]{1,0,3,2:T(4,128)} %get-tuple-element.440, f32[1,704,2,64]{1,0,3,2:T(1,128)S(1)} %copy.151, s32[]{:T(128)S(6)} %copy.177, s32[]{:T(128)} %constant.60.clone.1..sunk, s32[]{:T(128)} %constant.60.clone.1..sunk, s32[]{:T(128)} %constant.60.clone.1..sunk) | dynamic-update-slice | bytes 720900 | tf_op jit(solution)/shard_map/while/body/jit(dynamic_update_index_in_dim)/dynamic_update_slice | solution.py:174
  565.3 8.4 %dynamic_update_slice.29 = f32[4,704,2,64]{1,0,3,2:T(4,128)} dynamic-update-slice(f32[4,704,2,64]{1,0,3,2:T(4,128)} %get-tuple-element.439, f32[1,704,2,64]{1,0,3,2:T(1,128)S(1)} %copy.150, s32[]{:T(128)S(6)} %copy.177, s32[]{:T(128)} %constant.60.clone.1..sunk, s32[]{:T(128)} %constant.60.clone.1..sunk, s32[]{:T(128)} %constant.60.clone.1..sunk) | dynamic-update-slice | bytes 720900 | tf_op jit(solution)/shard_map/while/body/jit(dynamic_update_index_in_dim)/dynamic_update_slice | solution.py:174
  631.7 20.8 %all-to-all-done.4 = bf16[8,64,1026]{2,1,0:T(8,128)(2,1)} async-done(((bf16[8,64,1026]{2,1,0:T(8,128)(2,1)}), bf16[8,64,1026]{2,1,0:T(8,128)(2,1)}, u32[]{:S(2)}, u32[]{:S(2)}) %all-to-all-start.4) | async-done | bytes 1050656 | tf_op jit(solution)/shard_map/all_to_all | solution.py:20
  655.6 54.0 %all-reduce.19.cloned.1.call-done = (bf16[2816,512]{1,0:T(8,128)(2,1)}, bf16[2816,512]{1,0:T(8,128)(2,1)}) async-done(((bf16[2816,512]{1,0:T(8,128)(2,1)}, bf16[2816,512]{1,0:T(8,128)(2,1)}), (bf16[2816,512]{1,0:T(8,128)(2,1)}, bf16[2816,512]{1,0:T(8,128)(2,1)})) %all-reduce.19.cloned.1.call-update) | async-done | bytes 5767184 | tf_op jit(solution)/shard_map/psum | solution.py:154
  726.5 8.1 %add_add_fusion.2 = f32[2816,512]{1,0:T(8,128)} fusion(bf16[4,704,512]{2,1,0:T(8,128)(2,1)S(1)} %copy-done.2, bf16[2816,512]{1,0:T(8,128)(2,1)} %get-tuple-element.256, f32[2816,512]{1,0:T(8,128)} %get-tuple-element.261, f32[2816]{0:T(1024)S(1)} %negate_multiply_fusion.1, f32[2816]{0:T(1024)S(1)} %multiply_multiply_fusion.5, ...), kind=kLoop, calls=%fused_computation.83 | loop fusion | flops 18743296 | bytes 20243456 | tf_op jit(solution)/shard_map/add | solution.py:193
  748.6 7.1 all-to-all-done.1
  (330 shorter events, 274.8 us)
Async XLA Ops:
  7.3 30.0 %copy-start.44 = (bf16[64,3,128]{2,0,1:T(8,128)(2,1)S(1)}, bf16[64,3,128]{2,0,1:T(8,128)(2,1)}, u32[]{:S(2)}) copy-start(bf16[64,3,128]{2,0,1:T(8,128)(2,1)} %param.22) | copy-start | bytes 147460
  7.3 287.7 %all-reduce.15.cloned.1.call-start = ((), (), s32[]{:S(2)}) async-start(), calls=%async_computation.5 | async-start | bytes 11534336 | tf_op jit(solution)/shard_map/psum | solution.py:146
  7.3 97.5 %copy-start.49 = (f32[32]{0:T(128)}, f32[32]{0:T(128)S(1)}, u32[]{:S(2)}) copy-start(f32[32]{0:T(128)S(1)} %multiply_exponential_fusion) | copy-start | bytes 388
  9.9 60.0 %copy-start.31 = (f32[2816]{0:T(1024)}, f32[2816]{0:T(1024)S(1)}, u32[]{:S(2)}) copy-start(f32[2816]{0:T(1024)S(1)} %div.47) | copy-start | bytes 33796
  37.1 34.2 %copy-start.41 = (f32[512]{0:T(512)}, f32[512]{0:T(512)S(1)}, u32[]{:S(2)}) copy-start(f32[512]{0:T(512)S(1)} %convert_element_type.198) | copy-start | bytes 6148
  37.3 34.1 %copy-start.37 = (f32[2816]{0:T(1024)}, f32[2816]{0:T(1024)S(1)}, u32[]{:S(2)}) copy-start(f32[2816]{0:T(1024)S(1)} %add.103) | copy-start | bytes 33796
  37.3 31.1 %copy-start.33 = (f32[2816]{0:T(1024)}, f32[2816]{0:T(1024)S(1)}, u32[]{:S(2)}) copy-start(f32[2816]{0:T(1024)S(1)} %rsqrt.20) | copy-start | bytes 33796
  186.5 250.5 %all-reduce.17.cloned.1.call-start = ((), (), s32[]{:S(2)}) async-start(), calls=%async_computation.6 | async-start | bytes 11534336 | tf_op jit(solution)/shard_map/psum | solution.py:163
  303.2 16.7 %copy-start.5 = (f32[2816,512]{1,0:T(8,128)}, f32[2816,512]{1,0:T(8,128)S(1)}, u32[]{:S(2)}) copy-start(f32[2816,512]{1,0:T(8,128)S(1)} %fusion.98) | copy-start | bytes 17301508
  340.6 96.4 %copy-start.36 = (f32[2816]{0:T(1024)S(1)}, f32[2816]{0:T(1024)}, u32[]{:S(2)}) copy-start(f32[2816]{0:T(1024)} %copy-done.35) | copy-start | bytes 33796
  343.1 100.2 %copy-start.40 = (f32[2816]{0:T(1024)S(1)}, f32[2816]{0:T(1024)}, u32[]{:S(2)}) copy-start(f32[2816]{0:T(1024)} %copy-done.39) | copy-start | bytes 33796
  443.3 12.7 %copy-start.10 = (bf16[4,704,512]{2,1,0:T(8,128)(2,1)S(1)}, bf16[4,704,512]{2,1,0:T(8,128)(2,1)}, u32[]{:S(2)}) copy-start(bf16[4,704,512]{2,1,0:T(8,128)(2,1)} %param.29) | copy-start | bytes 8650756
  450.4 151.2 %all-to-all-start.3 = ((bf16[8,1,64]{2,1,0:T(2,128)(2,1)}), bf16[8,1,64]{2,1,0:T(2,128)(2,1)S(1)}, u32[]{:S(2)}, u32[]{:S(2)}) async-start(bf16[8,1,64]{2,1,0:T(2,128)(2,1)} %convert_element_type.240), calls=%async_computation.3 | async-start | bytes 8192 | tf_op jit(solution)/shard_map/all_to_all | solution.py:20
  456.0 253.6 %all-reduce.19.cloned.1.call-start = ((), (), s32[]{:S(2)}) async-start(), calls=%async_computation.7 | async-start | bytes 11534336 | tf_op jit(solution)/shard_map/psum | solution.py:154
  601.6 17.4 %all-to-all-start.2 = ((bf16[8,16,512]{2,1,0:T(8,128)(2,1)}), bf16[8,16,512]{2,1,0:T(8,128)(2,1)}, u32[]{:S(2)}, u32[]{:S(2)}) async-start(bf16[8,16,512]{2,1,0:T(8,128)(2,1)} %bitcast.31), calls=%async_computation.2 | async-start | bytes 262144 | tf_op jit(solution)/shard_map/all_to_all | solution.py:20
  607.5 7.9 %copy-start.28 = (bf16[512,512]{1,0:T(8,128)(2,1)S(1)}, bf16[512,512]{1,0:T(8,128)(2,1)}, u32[]{:S(2)}) copy-start(bf16[512,512]{1,0:T(8,128)(2,1)} %convolution_convert_fusion.3) | copy-start | bytes 1572868
  612.8 12.2 %copy-start.12 = (bf16[2816,512]{1,0:T(8,128)(2,1)S(1)}, bf16[2816,512]{1,0:T(8,128)(2,1)}, u32[]{:S(2)}) copy-start(bf16[2816,512]{1,0:T(8,128)(2,1)} %copy-done.11) | copy-start | bytes 8650756
  619.0 33.6 %all-to-all-start.4 = ((bf16[8,64,1026]{2,1,0:T(8,128)(2,1)}), bf16[8,64,1026]{2,1,0:T(8,128)(2,1)}, u32[]{:S(2)}, u32[]{:S(2)}) async-start(bf16[8,64,1026]{2,1,0:T(8,128)(2,1)} %concatenate.60), calls=%async_computation.4 | async-start | bytes 2359296 | tf_op jit(solution)/shard_map/all_to_all | solution.py:20
  624.9 84.6 %copy-start.32 = (f32[2816]{0:T(1024)S(1)}, f32[2816]{0:T(1024)}, u32[]{:S(2)}) copy-start(f32[2816]{0:T(1024)} %copy-done.31) | copy-start | bytes 33796
  625.0 84.6 %copy-start.42 = (f32[512]{0:T(512)S(1)}, f32[512]{0:T(512)}, u32[]{:S(2)}) copy-start(f32[512]{0:T(512)} %copy-done.41) | copy-start | bytes 6148
  628.2 81.4 %copy-start.2 = (bf16[4,704,512]{2,1,0:T(8,128)(2,1)S(1)}, bf16[4,704,512]{2,1,0:T(8,128)(2,1)}, u32[]{:S(2)}) copy-start(bf16[4,704,512]{2,1,0:T(8,128)(2,1)} %param.17) | copy-start | bytes 8650756
  720.7 15.3 %all-to-all-start = ((bf16[8,1,64]{2,1,0:T(2,128)(2,1)}), bf16[8,1,64]{2,1,0:T(2,128)(2,1)S(1)}, u32[]{:S(2)}, u32[]{:S(2)}) async-start(bf16[8,1,64]{2,1,0:T(2,128)(2,1)} %convert_element_type.238), calls=%async_computation | async-start | bytes 8192 | tf_op jit(solution)/shard_map/all_to_all | solution.py:20
  726.5 8.3 %copy-start.21 = (bf16[8,64,384]{2,1,0:T(8,128)(2,1)S(1)}, bf16[8,64,384]{2,1,0:T(8,128)(2,1)}, u32[]{:S(2)}) copy-start(bf16[8,64,384]{2,1,0:T(8,128)(2,1)} %concatenate.55) | copy-start | bytes 1179652
  736.0 19.8 %all-to-all-start.1 = ((bf16[8,64,385]{2,1,0:T(8,128)(2,1)}), bf16[8,64,385]{2,1,0:T(8,128)(2,1)S(1)}, u32[]{:S(2)}, u32[]{:S(2)}) async-start(bf16[8,64,385]{2,1,0:T(8,128)(2,1)} %pad_maximum_fusion.5), calls=%async_computation.1 | async-start | bytes 1048576 | tf_op jit(solution)/shard_map/all_to_all | solution.py:20
  (49 other events, 167.2 us)
Sparse Core Ops, SparseCore 0:
  186.6 108.3 all-reduce.14
  325.7 111.2 all-reduce.16
  597.6 111.8 all-reduce.18
where the time goes:
time: 773 us; the launch traced here: 764 us
  waiting for transfers between devices  217 us (28%)
  local copies, waits for them, and re-layouts  151 us (20%)
  blocking collectives  150 us (19%)
  other arithmetic  107 us (14%)
  matrix products  92.4 us (12%)
  starting transfers between devices  29.4 us (4%)
  between operations  15.5 us (2%)
    psum x1, waiting for transfers between devices, run_layer(): ffn_in_grad = lax.psum(ffn_in_part, 'tensor')  93.9 us
    dynamic_update_slice x16, local copies, waits for them, and re-layouts, run_layer(): lax.map(attend_backward, (queries, key_rows, value_rows, seg_count, log_t...  70.8 us
    psum x1, waiting for transfers between devices, run_layer(): lax.psum(ffn_part.astype(jnp.bfloat16), 'tensor').astype(jnp.float32)  54 us
    psum x1, waiting for transfers between devices, run_layer(): attn_full = lax.psum(attn_part, 'tensor')  41.4 us
    all_gather x1, blocking collectives, local(): lax.all_gather(down_weight, 'dp', axis=0, tiled=True)  33.4 us
    all_gather x1, blocking collectives, local(): lax.all_gather(up_weight, 'dp', axis=0, tiled=True)  31.8 us
    all_gather x1, blocking collectives, local(): lax.all_gather(qkv_weight, 'dp', axis=0, tiled=True)  31 us
    all_gather x1, blocking collectives, local(): lax.all_gather(out_weight, 'dp', axis=0, tiled=True)  30.7 us
  transfers between devices with their start and end apart: 8, of which 5 were waited for; matrix products, arithmetic and copies ran while one was open for 26% of the time, Pallas kernels for 0%

commit v1 on v0

--- a/solution.py
+++ b/solution.py
@@ -143,7 +143,8 @@
     mixed_rows, log_total = lax.map(attend_forward, (queries, key_rows, value_rows, seg_count))
     mixed_flat = mixed_rows.reshape(token_rows, local_width)
     attn_part = jnp.dot(mixed_flat, w_out, preferred_element_type=jnp.float32)
-    attn_full = lax.psum(attn_part, "tensor")
+    parts = lax.all_gather(attn_part, "tensor", axis=0, tiled=False)
+    attn_full = parts.sum(axis=0)
     residual = inputs + attn_full
     normed_two, norm_two_pull = jax.vjp(normalize, residual, gain_two, shift_two)
     ffn_in = normed_two.astype(jnp.bfloat16)

time: 773 us -> 848 us (1.097)
  waiting for transfers between devices: 217 us -> 247 us
  matrix products: 92.4 us -> 117 us
  other arithmetic: 107 us -> 121 us
  local copies, waits for them, and re-layouts: 151 us -> 162 us
    all_gather x0 -> x1, waiting for transfers between devices: none -> 73.5 us  [run_layer(): parts = lax.all_gather(attn_part, 'tensor', axis=0, tiled=False)]
    psum x1 -> x0, waiting for transfers between devices: 41.4 us -> none  [run_layer(): attn_full = lax.psum(attn_part, 'tensor')]
    reduce_sum x0 -> x1, other arithmetic: none -> 14.3 us  [run_layer(): attn_full = parts.sum(axis=0)]
    dot_general x4, matrix products: 4.6 us -> 16.7 us  [attend_backward(): jnp.einsum('hqk,qhd->khd', attention_probs.astype(jnp.bfloat16), out_grad...]
  transfers between devices with their start and end apart: 8 -> 8, of which waited for: 5 -> 6; matrix products, arithmetic and copies ran while one was open for 26% -> 7% of each run, Pallas kernels for 0% -> 0%
where the time goes in v1:
time: 848 us; the launch traced here: 840 us
  waiting for transfers between devices  247 us (29%)
  local copies, waits for them, and re-layouts  162 us (19%)
  blocking collectives  150 us (18%)
  other arithmetic  121 us (14%)
  matrix products  117 us (14%)
  starting transfers between devices  27 us (3%)
  between operations  15.5 us (2%)
    psum x1, waiting for transfers between devices, run_layer(): ffn_in_grad = lax.psum(ffn_in_part, 'tensor')  92.3 us
    all_gather x1, waiting for transfers between devices, run_layer(): parts = lax.all_gather(attn_part, 'tensor', axis=0, tiled=False)  73.5 us
    dynamic_update_slice x16, local copies, waits for them, and re-layouts, run_layer(): lax.map(attend_backward, (queries, key_rows, value_rows, seg_count, log_t...  70.7 us
    psum x1, waiting for transfers between devices, run_layer(): lax.psum(ffn_part.astype(jnp.bfloat16), 'tensor').astype(jnp.float32)  53.9 us
    all_gather x1, blocking collectives, local(): lax.all_gather(down_weight, 'dp', axis=0, tiled=True)  33.4 us
    all_gather x1, blocking collectives, local(): lax.all_gather(up_weight, 'dp', axis=0, tiled=True)  31.8 us
    all_gather x1, blocking collectives, local(): lax.all_gather(qkv_weight, 'dp', axis=0, tiled=True)  31.1 us
    all_gather x1, blocking collectives, local(): lax.all_gather(out_weight, 'dp', axis=0, tiled=True)  30.6 us
  transfers between devices with their start and end apart: 8, of which 6 were waited for; matrix products, arithmetic and copies ran while one was open for 7% of the time, Pallas kernels for 0%

profile of v1, /device:TPU:0, one launch (start us, length us, event | category | flops | bytes accessed | tf_op | source)
XLA Modules:
  0.0 840.2 jit_solution(8690211813706925747)
XLA Ops:
  15.5 23.4 %all-reduce.9 = (bf16[512]{0:T(512)(128)(2,1)S(1)}, bf16[512]{0:T(512)(128)(2,1)S(1)}, bf16[512]{0:T(512)(128)(2,1)S(1)}, bf16[512]{0:T(512)(128)(2,1)S(1)}, bf16[512]{0:T(512)(128)(2,1)S(1)}) all-reduce(bf16[512]{0:T(512)(128)(2,1)S(1)} %dynamic-update-slice.3, ...), channel_id=1, replica_groups=mesh['dp'=8,'tensor'=4] {'dp'}, use_global_device_ids=true, to_apply=%add.7 | all-reduce | flops 2560 | bytes 10240
  39.0 31.1 %all_gather.35 = bf16[512,3,128]{2,0,1:T(8,128)(2,1)S(1)} all-gather(bf16[64,3,128]{2,0,1:T(8,128)(2,1)S(1)} %copy-done.42), channel_id=1, replica_groups=mesh['dp'=8,'tensor'=4] {'dp'}, dimensions={0}, use_global_device_ids=true | all-gather | bytes 442368 | tf_op jit(solution)/shard_map/all_gather | solution.py:229
  114.8 31.6 %while.26 = (s32[]{:T(128)}, bf16[4,704,2,64]{1,3,2,0:T(8,128)(2,1)}, f32[4,2,704]{2,1,0:T(2,128)}, bf16[4,704,2,64]{1,3,2,0:T(8,128)(2,1)}, s32[4]{0:T(128)S(1)...) while((s32[]{:T(128)}, bf16[4,704,2,64]{1,3,2,0:T(8,128)(2,1)}, ...), condition=%wide.region_5.6_spmd, body=%wide.region_2.5_spmd.sunk | while | flops 263757120 | bytes 14713317 | solution.py:143
  151.7 30.6 %all_gather.36 = bf16[128,512]{1,0:T(8,128)(2,1)S(1)} all-gather(bf16[16,512]{1,0:T(8,128)(2,1)S(1)} %copy-done.43), channel_id=1, replica_groups=mesh['dp'=8,'tensor'=4] {'dp'}, dimensions={0}, use_global_device_ids=true | all-gather | bytes 147456 | tf_op jit(solution)/shard_map/all_gather | solution.py:230
  188.8 31.8 %all_gather.41 = bf16[512,512]{1,0:T(8,128)(2,1)S(1)} all-gather(bf16[64,512]{1,0:T(8,128)(2,1)} %param.26), channel_id=1, replica_groups=mesh['dp'=8,'tensor'=4] {'dp'}, dimensions={0}, use_global_device_ids=true | all-gather | bytes 589824 | tf_op jit(solution)/shard_map/all_gather | solution.py:231
  220.7 33.4 %all_gather.43 = bf16[512,512]{1,0:T(8,128)(2,1)} all-gather(bf16[64,512]{1,0:T(8,128)(2,1)} %param.28), channel_id=1, replica_groups=mesh['dp'=8,'tensor'=4] {'dp'}, dimensions={0}, use_global_device_ids=true | all-gather | bytes 589824 | tf_op jit(solution)/shard_map/all_gather | solution.py:233
  254.1 73.5 %all-gather.3.cloned.1.call-done = f32[11264,512]{1,0:T(8,128)} async-done(((f32[2816,512]{1,0:T(8,128)}), f32[11264,512]{1,0:T(8,128)}) %all-gather.3.cloned.1.call-update) | async-done | bytes 23068688 | tf_op jit(solution)/shard_map/all_gather | solution.py:146
  327.6 14.3 %reduce_sum.204 = f32[2816,512]{1,0:T(8,128)} reduce(f32[4,2816,512]{2,1,0:T(8,128)} %bitcast.209, f32[]{:T(128)} %constant.62.clone.1), dimensions={0}, to_apply=%region_6.7 | reduce | flops 4325376 | bytes 28835844 | tf_op jit(solution)/shard_map/reduce_sum | solution.py:147
  360.5 16.5 %fusion.89 = (bf16[512]{0:T(512)(128)(2,1)}, bf16[2816,512]{1,0:T(8,128)(2,1)S(1)}, f32[2816,512]{1,0:T(8,128)}) fusion(f32[2816,512]{1,0:T(8,128)S(1)} %fusion.97, f32[512]{0:T(512)S(1)} %copy-done.45, bf16[2816,512]{1,0:T(8,128)(2,1)S(1)} %bitcast.213, bf16[512,512]{1,0:T(8,128)(2,1)S(1)} %copy-done.27), kind=kOutput, calls=%fused_computation.167 | convolution fusion | flops 1583087104 | bytes 17828864 | tf_op jit(solution)/shard_map/nd,fd->nf/dot_general | solution.py:159
  387.5 6.9 multiply_convert_fusion.1
  401.7 92.3 %all-reduce.14.cloned.1.call-done = f32[2816,512]{1,0:T(8,128)} async-done(((f32[2816,512]{1,0:T(8,128)}), f32[2816,512]{1,0:T(8,128)}) %all-reduce.14.cloned.1.call-update) | async-done | bytes 5767184 | tf_op jit(solution)/shard_map/psum | solution.py:164
  494.1 6.4 multiply_reduce_fusion.1
  518.2 130.6 %while.27 = (s32[]{:T(128)}, f32[4,704,2,64]{1,0,3,2:T(4,128)}, f32[4,704,2,64]{1,0,3,2:T(4,128)}, bf16[4,704,2,64]{1,3,2,0:T(8,128)(2,1)}, bf16[4,704,2,64]{1,3...) while((s32[]{:T(128)}, f32[4,704,2,64]{1,0,3,2:T(4,128)}, ...), condition=%wide.region_15.16_spmd, body=%wide.region_13.15_spmd.sunk | while | flops 647273792 | bytes 53358636 | solution.py:175
  528.1 8.4 %dynamic_update_slice.30 = f32[4,704,2,64]{1,0,3,2:T(4,128)} dynamic-update-slice(f32[4,704,2,64]{1,0,3,2:T(4,128)} %get-tuple-element.440, f32[1,704,2,64]{1,0,3,2:T(1,128)S(1)} %copy.152, s32[]{:T(128)} %get-tuple-element.438, s32[]{:T(128)} %constant.60.clone.1..sunk, s32[]{:T(128)} %constant.60.clone.1..sunk, s32[]{:T(128)} %constant.60.clone.1..sunk) | dynamic-update-slice | bytes 720900 | tf_op jit(solution)/shard_map/while/body/jit(dynamic_update_index_in_dim)/dynamic_update_slice | solution.py:175
  538.4 8.4 %dynamic_update_slice.29 = f32[4,704,2,64]{1,0,3,2:T(4,128)} dynamic-update-slice(f32[4,704,2,64]{1,0,3,2:T(4,128)} %get-tuple-element.439, f32[1,704,2,64]{1,0,3,2:T(1,128)S(1)} %copy.151, s32[]{:T(128)} %get-tuple-element.438, s32[]{:T(128)} %constant.60.clone.1..sunk, s32[]{:T(128)} %constant.60.clone.1..sunk, s32[]{:T(128)} %constant.60.clone.1..sunk) | dynamic-update-slice | bytes 720900 | tf_op jit(solution)/shard_map/while/body/jit(dynamic_update_index_in_dim)/dynamic_update_slice | solution.py:175
  560.7 8.4 %dynamic_update_slice.30 = f32[4,704,2,64]{1,0,3,2:T(4,128)} dynamic-update-slice(f32[4,704,2,64]{1,0,3,2:T(4,128)} %get-tuple-element.440, f32[1,704,2,64]{1,0,3,2:T(1,128)S(1)} %copy.152, s32[]{:T(128)} %get-tuple-element.438, s32[]{:T(128)} %constant.60.clone.1..sunk, s32[]{:T(128)} %constant.60.clone.1..sunk, s32[]{:T(128)} %constant.60.clone.1..sunk) | dynamic-update-slice | bytes 720900 | tf_op jit(solution)/shard_map/while/body/jit(dynamic_update_index_in_dim)/dynamic_update_slice | solution.py:175
  571.0 8.4 %dynamic_update_slice.29 = f32[4,704,2,64]{1,0,3,2:T(4,128)} dynamic-update-slice(f32[4,704,2,64]{1,0,3,2:T(4,128)} %get-tuple-element.439, f32[1,704,2,64]{1,0,3,2:T(1,128)S(1)} %copy.151, s32[]{:T(128)} %get-tuple-element.438, s32[]{:T(128)} %constant.60.clone.1..sunk, s32[]{:T(128)} %constant.60.clone.1..sunk, s32[]{:T(128)} %constant.60.clone.1..sunk) | dynamic-update-slice | bytes 720900 | tf_op jit(solution)/shard_map/while/body/jit(dynamic_update_index_in_dim)/dynamic_update_slice | solution.py:175
  593.3 8.4 %dynamic_update_slice.30 = f32[4,704,2,64]{1,0,3,2:T(4,128)} dynamic-update-slice(f32[4,704,2,64]{1,0,3,2:T(4,128)} %get-tuple-element.440, f32[1,704,2,64]{1,0,3,2:T(1,128)S(1)} %copy.152, s32[]{:T(128)} %get-tuple-element.438, s32[]{:T(128)} %constant.60.clone.1..sunk, s32[]{:T(128)} %constant.60.clone.1..sunk, s32[]{:T(128)} %constant.60.clone.1..sunk) | dynamic-update-slice | bytes 720900 | tf_op jit(solution)/shard_map/while/body/jit(dynamic_update_index_in_dim)/dynamic_update_slice | solution.py:175
  603.6 8.4 %dynamic_update_slice.29 = f32[4,704,2,64]{1,0,3,2:T(4,128)} dynamic-update-slice(f32[4,704,2,64]{1,0,3,2:T(4,128)} %get-tuple-element.439, f32[1,704,2,64]{1,0,3,2:T(1,128)S(1)} %copy.151, s32[]{:T(128)} %get-tuple-element.438, s32[]{:T(128)} %constant.60.clone.1..sunk, s32[]{:T(128)} %constant.60.clone.1..sunk, s32[]{:T(128)} %constant.60.clone.1..sunk) | dynamic-update-slice | bytes 720900 | tf_op jit(solution)/shard_map/while/body/jit(dynamic_update_index_in_dim)/dynamic_update_slice | solution.py:175
  625.9 8.4 %dynamic_update_slice.30 = f32[4,704,2,64]{1,0,3,2:T(4,128)} dynamic-update-slice(f32[4,704,2,64]{1,0,3,2:T(4,128)} %get-tuple-element.440, f32[1,704,2,64]{1,0,3,2:T(1,128)S(1)} %copy.152, s32[]{:T(128)} %get-tuple-element.438, s32[]{:T(128)} %constant.60.clone.1..sunk, s32[]{:T(128)} %constant.60.clone.1..sunk, s32[]{:T(128)} %constant.60.clone.1..sunk) | dynamic-update-slice | bytes 720900 | tf_op jit(solution)/shard_map/while/body/jit(dynamic_update_index_in_dim)/dynamic_update_slice | solution.py:175
  636.2 8.4 %dynamic_update_slice.29 = f32[4,704,2,64]{1,0,3,2:T(4,128)} dynamic-update-slice(f32[4,704,2,64]{1,0,3,2:T(4,128)} %get-tuple-element.439, f32[1,704,2,64]{1,0,3,2:T(1,128)S(1)} %copy.151, s32[]{:T(128)} %get-tuple-element.438, s32[]{:T(128)} %constant.60.clone.1..sunk, s32[]{:T(128)} %constant.60.clone.1..sunk, s32[]{:T(128)} %constant.60.clone.1..sunk) | dynamic-update-slice | bytes 720900 | tf_op jit(solution)/shard_map/while/body/jit(dynamic_update_index_in_dim)/dynamic_update_slice | solution.py:175
  714.3 20.8 %all-to-all-done.4 = bf16[8,64,1026]{2,1,0:T(8,128)(2,1)} async-done(((bf16[8,64,1026]{2,1,0:T(8,128)(2,1)}), bf16[8,64,1026]{2,1,0:T(8,128)(2,1)}, u32[]{:S(2)}, u32[]{:S(2)}) %all-to-all-start.4) | async-done | bytes 1050656 | tf_op jit(solution)/shard_map/all_to_all | solution.py:20
  738.1 53.9 %all-reduce.16.cloned.1.call-done = (bf16[2816,512]{1,0:T(8,128)(2,1)}, bf16[2816,512]{1,0:T(8,128)(2,1)}) async-done(((bf16[2816,512]{1,0:T(8,128)(2,1)}, bf16[2816,512]{1,0:T(8,128)(2,1)}), (bf16[2816,512]{1,0:T(8,128)(2,1)}, bf16[2816,512]{1,0:T(8,128)(2,1)})) %all-reduce.16.cloned.1.call-update) | async-done | bytes 5767184 | tf_op jit(solution)/shard_map/psum | solution.py:155
  818.9 11.1 %add_add_fusion.2 = (f32[2816,512]{1,0:T(8,128)}, bf16[2816,512]{1,0:T(8,128)(2,1)}) fusion(bf16[4,704,512]{2,1,0:T(8,128)(2,1)S(1)} %copy-done.2, bf16[2816,512]{1,0:T(8,128)(2,1)} %get-tuple-element.256, f32[2816,512]{1,0:T(8,128)} %copy-done.4, f32[2816]{0:T(1024)S(1)} %negate_multiply_fusion.1, f32[2816]{0:T(1024)S(1)} %multiply_multiply_fusion.5, ...), kind=kLoop, calls=%fused_computation.84 | loop fusion | flops 24510464 | bytes 31777792 | tf_op jit(solution)/shard_map/add | solution.py:194
  (323 shorter events, 310.4 us)
Async XLA Ops:
  7.2 63.0 %copy-start.1 = (bf16[4,704,512]{2,1,0:T(8,128)(2,1)S(1)}, bf16[4,704,512]{2,1,0:T(8,128)(2,1)}, u32[]{:S(2)}) copy-start(bf16[4,704,512]{2,1,0:T(8,128)(2,1)} %param.17) | copy-start | bytes 8650756
  7.3 31.8 %copy-start.42 = (bf16[64,3,128]{2,0,1:T(8,128)(2,1)S(1)}, bf16[64,3,128]{2,0,1:T(8,128)(2,1)}, u32[]{:S(2)}) copy-start(bf16[64,3,128]{2,0,1:T(8,128)(2,1)} %param.22) | copy-start | bytes 147460
  7.3 320.3 %all-gather.3.cloned.1.call-start = ((), (), s32[]{:S(2)}) async-start(), calls=%async_computation.6 | async-start | bytes 28835840 | tf_op jit(solution)/shard_map/all_gather | solution.py:146
  12.9 60.3 %copy-start.29 = (f32[2816]{0:T(1024)}, f32[2816]{0:T(1024)S(1)}, u32[]{:S(2)}) copy-start(f32[2816]{0:T(1024)S(1)} %div.49) | copy-start | bytes 33796
  12.9 85.3 %copy-start.47 = (f32[32]{0:T(128)}, f32[32]{0:T(128)S(1)}, u32[]{:S(2)}) copy-start(f32[32]{0:T(128)S(1)} %multiply_exponential_fusion) | copy-start | bytes 388
  38.9 34.3 %copy-start.39 = (f32[512]{0:T(512)}, f32[512]{0:T(512)S(1)}, u32[]{:S(2)}) copy-start(f32[512]{0:T(512)S(1)} %convert_element_type.200) | copy-start | bytes 6148
  39.0 34.2 %copy-start.36 = (f32[2816]{0:T(1024)}, f32[2816]{0:T(1024)S(1)}, u32[]{:S(2)}) copy-start(f32[2816]{0:T(1024)S(1)} %add.108) | copy-start | bytes 33796
  39.0 31.1 %copy-start.33 = (f32[2816]{0:T(1024)}, f32[2816]{0:T(1024)S(1)}, u32[]{:S(2)}) copy-start(f32[2816]{0:T(1024)S(1)} %rsqrt.20) | copy-start | bytes 33796
  114.8 37.0 %copy-start.43 = (bf16[16,512]{1,0:T(8,128)(2,1)S(1)}, bf16[16,512]{1,0:T(8,128)(2,1)}, u32[]{:S(2)}) copy-start(bf16[16,512]{1,0:T(8,128)(2,1)} %param.23) | copy-start | bytes 49156
  186.9 307.1 %all-reduce.14.cloned.1.call-start = ((), (), s32[]{:S(2)}) async-start(), calls=%async_computation.5 | async-start | bytes 11534336 | tf_op jit(solution)/shard_map/psum | solution.py:164
  356.6 20.4 %copy-start.9 = (bf16[2816,512]{1,0:T(8,128)(2,1)}, bf16[2816,512]{1,0:T(8,128)(2,1)S(1)}, u32[]{:S(2)}) copy-start(bf16[2816,512]{1,0:T(8,128)(2,1)S(1)} %add_convert_fusion.2) | copy-start | bytes 8650756
  399.2 94.8 %copy-start.32 = (f32[2816]{0:T(1024)S(1)}, f32[2816]{0:T(1024)}, u32[]{:S(2)}) copy-start(f32[2816]{0:T(1024)} %copy-done.31) | copy-start | bytes 33796
  401.7 98.7 %copy-start.38 = (f32[2816]{0:T(1024)S(1)}, f32[2816]{0:T(1024)}, u32[]{:S(2)}) copy-start(f32[2816]{0:T(1024)} %add.116) | copy-start | bytes 33796
  669.5 14.5 %all-to-all-start.3 = ((bf16[8,1,64]{2,1,0:T(2,128)(2,1)}), bf16[8,1,64]{2,1,0:T(2,128)(2,1)S(1)}, u32[]{:S(2)}, u32[]{:S(2)}) async-start(bf16[8,1,64]{2,1,0:T(2,128)(2,1)} %convert_element_type.242), calls=%async_computation.3 | async-start | bytes 8192 | tf_op jit(solution)/shard_map/all_to_all | solution.py:20
  675.0 117.0 %all-reduce.16.cloned.1.call-start = ((), (), s32[]{:S(2)}) async-start(), calls=%async_computation.7 | async-start | bytes 11534336 | tf_op jit(solution)/shard_map/psum | solution.py:155
  684.0 17.4 %all-to-all-start.2 = ((bf16[8,16,512]{2,1,0:T(8,128)(2,1)}), bf16[8,16,512]{2,1,0:T(8,128)(2,1)}, u32[]{:S(2)}, u32[]{:S(2)}) async-start(bf16[8,16,512]{2,1,0:T(8,128)(2,1)} %bitcast.33), calls=%async_computation.2 | async-start | bytes 262144 | tf_op jit(solution)/shard_map/all_to_all | solution.py:20
  701.5 33.6 %all-to-all-start.4 = ((bf16[8,64,1026]{2,1,0:T(8,128)(2,1)}), bf16[8,64,1026]{2,1,0:T(8,128)(2,1)}, u32[]{:S(2)}, u32[]{:S(2)}) async-start(bf16[8,64,1026]{2,1,0:T(8,128)(2,1)} %concatenate.60), calls=%async_computation.4 | async-start | bytes 2359296 | tf_op jit(solution)/shard_map/all_to_all | solution.py:20
  707.5 84.5 %copy-start.30 = (f32[2816]{0:T(1024)S(1)}, f32[2816]{0:T(1024)}, u32[]{:S(2)}) copy-start(f32[2816]{0:T(1024)} %copy-done.29) | copy-start | bytes 33796
  707.5 84.5 %copy-start.40 = (f32[512]{0:T(512)S(1)}, f32[512]{0:T(512)}, u32[]{:S(2)}) copy-start(f32[512]{0:T(512)} %copy-done.39) | copy-start | bytes 6148
  710.7 81.3 %copy-start.2 = (bf16[4,704,512]{2,1,0:T(8,128)(2,1)S(1)}, bf16[4,704,512]{2,1,0:T(8,128)(2,1)}, u32[]{:S(2)}) copy-start(bf16[4,704,512]{2,1,0:T(8,128)(2,1)} %param.17) | copy-start | bytes 8650756
  711.1 86.9 %copy-start.37 = (f32[2816]{0:T(1024)S(1)}, f32[2816]{0:T(1024)}, u32[]{:S(2)}) copy-start(f32[2816]{0:T(1024)} %copy-done.36) | copy-start | bytes 33796
  712.2 85.8 %copy-start.34 = (f32[2816]{0:T(1024)S(1)}, f32[2816]{0:T(1024)}, u32[]{:S(2)}) copy-start(f32[2816]{0:T(1024)} %copy-done.33) | copy-start | bytes 33796
  803.5 11.9 %all-to-all-start = ((bf16[8,1,64]{2,1,0:T(2,128)(2,1)}), bf16[8,1,64]{2,1,0:T(2,128)(2,1)S(1)}, u32[]{:S(2)}, u32[]{:S(2)}) async-start(bf16[8,1,64]{2,1,0:T(2,128)(2,1)} %convert_element_type.240), calls=%async_computation | async-start | bytes 8192 | tf_op jit(solution)/shard_map/all_to_all | solution.py:20
  815.4 16.5 %all-to-all-start.1 = ((bf16[8,64,385]{2,1,0:T(8,128)(2,1)}), bf16[8,64,385]{2,1,0:T(8,128)(2,1)S(1)}, u32[]{:S(2)}, u32[]{:S(2)}) async-start(bf16[8,64,385]{2,1,0:T(8,128)(2,1)} %pad_maximum_fusion.5), calls=%async_computation.1 | async-start | bytes 1048576 | tf_op jit(solution)/shard_map/all_to_all | solution.py:20
  (44 other events, 279.0 us)
Sparse Core Ops, SparseCore 0:
  187.0 140.4 all-gather.2
  382.9 111.0 all-reduce.13
  680.1 111.8 all-reduce.15
